TPU v7x, 256 devices: a whole 4x4x8 slice. The times are simulated.
256 devices in a mesh: dp: 16 (over y, x), vocab: 16 (over z, core).
Axes of the slice: x: 4, y: 4, z: 8, core: 2. Of those that a mesh axis runs over, the one named last changes fastest.
Arguments:
- hidden: bfloat16 [256, 128, 4096], P('vocab', None, 'dp'), may hold values from -6 to 6
- weights: bfloat16 [65536, 4096], P('vocab', 'dp'), may hold values from -0.09375 to 0.09375
- bias: float32 [65536], P('vocab'), may hold values from -4 to 4
- first_moment: bfloat16 [65536, 4096], P('vocab', 'dp'), may hold values from -6 to 6
- second_moment: bfloat16 [65536, 4096], P('vocab', 'dp'), may hold values from 0.049804688 to 2
- rep_cot: bfloat16 [256, 16, 512], P(None, 'vocab'), may hold values from -768 to 768
- active_blocks: int32 [256, 16, 4], P(None, 'vocab'), may hold values from 0 to 31, as said below
- block_counts: int32 [256, 16], replicated, may hold values from 0 to 4, as said below
- passage_len: int32 [256], replicated, may hold values from 16 to 128, as said below
Outputs:
- reps: float32 [16, 16, 4, 512], P('dp', 'vocab')
- grad_hidden: bfloat16 [256, 128, 4096], P('vocab', None, 'dp')
- new_first: bfloat16 [65536, 4096], P('vocab', 'dp')
- new_second: bfloat16 [65536, 4096], P('vocab', 'dp')
Inputs may be any that keep to these rules, and one draw needn't show every extreme that they name: `block_counts`: within each batch of 16 passages, every owner has between max(1, 2) and 4 live passages, and in every batch some owner has exactly 4; some passage at each owner of each batch has count 4. `active_blocks`: the 4 block numbers of one passage at one owner are distinct. `passage_len`: every batch has a passage of length 128.
All inputs are finite; a program needn't handle non-finite values.
Results may differ from a plain program's by a relative error of at most 0.012.
Values may be sent and summed in bfloat16 or wider, within the bound.
No kernel may reach another device: no remote copies, remote signals or barrier semaphores. Data moves between devices by JAX's collectives and lax.ppermute only.
A program may use at most 128 MiB of HBM per device.

v0:
```python
import jax
import jax.numpy as jnp
from jax import lax
from jax.sharding import PartitionSpec as P

BLOCK = 128
OWN_BLOCKS = 32
SLOT_BLOCKS = 4
OWN_SLOTS = 4


beta_one = 0.9
beta_two = 0.999


def slot_tables(block_counts, batches, owners, per_batch, slot_total):
    live_mask = (block_counts > 0).astype(jnp.int32).reshape(batches, per_batch, owners)
    slot_rank = jnp.cumsum(live_mask, axis=1, dtype=jnp.int32) - live_mask
    slot_place = jnp.arange(slot_total, dtype=jnp.int32)
    chosen = (live_mask[:, :, :, None] == 1) & (
        slot_rank[:, :, :, None] == slot_place[None, None, None, :]
    )
    return jnp.transpose(chosen, (0, 2, 3, 1)).astype(jnp.int32)


def slot_info(onehot, ids_col, counts_col, lengths, plen_size, block_size):
    slot_ids = jnp.sum(onehot[:, :, :, None] * ids_col[:, None, :, :], axis=2)
    slot_count = jnp.sum(onehot * counts_col[:, None, :], axis=2)
    slot_len = jnp.sum(onehot * lengths[:, None, :], axis=2)
    filled = jnp.sum(onehot, axis=2)
    divisor = jnp.where(filled > 0, slot_len, 1).astype(jnp.float32)
    token_ok = jnp.arange(plen_size, dtype=jnp.int32)[None, None, :] < slot_len[:, :, None]
    col_block = jnp.arange(slot_ids.shape[2] * block_size, dtype=jnp.int32) // block_size
    col_ok = col_block[None, None, :] < slot_count[:, :, None]
    return (slot_ids, divisor, token_ok, col_ok)


def activate(logits, bias_cols, cot, token_ok, col_ok, divisor):
    shifted = logits + bias_cols[:, :, None, :]
    softened = jax.nn.softplus(shifted)
    kept_mask = (token_ok[:, :, :, None] & col_ok[:, :, None, :]).astype(jnp.float32)
    pool_weight = kept_mask / divisor[:, :, None, None]
    pooled = jnp.sum(jnp.log1p(softened) * pool_weight, axis=2)
    slope = (cot[:, :, None, :] * pool_weight * jax.nn.sigmoid(shifted) / (1.0 + softened)).astype(
        jnp.bfloat16
    )
    return (pooled, slope)


def shards(
    hidden,
    weights,
    bias,
    first_moment,
    second_moment,
    rep_cot,
    active_blocks,
    block_counts,
    passage_len,
):
    owners = lax.axis_size("vocab")
    feature_parts = lax.axis_size("dp")
    per_batch, plen_size, dslice = hidden.shape
    col_width = SLOT_BLOCKS * BLOCK
    my_batch = lax.axis_index("vocab")
    chosen = slot_tables(block_counts, owners, owners, per_batch, OWN_SLOTS)
    my_slots = lax.dynamic_index_in_dim(chosen, my_batch, 0, keepdims=False)
    pick_rows = my_slots.reshape(owners * OWN_SLOTS, per_batch).astype(jnp.bfloat16)
    outgoing = jnp.dot(
        pick_rows, hidden.reshape(per_batch, plen_size * dslice), preferred_element_type=jnp.float32
    )
    outgoing = outgoing.astype(jnp.bfloat16).reshape(owners, OWN_SLOTS, plen_size, dslice)
    arrived = lax.all_to_all(outgoing, "vocab", split_axis=0, concat_axis=0, tiled=True)
    onehot = lax.dynamic_index_in_dim(chosen, my_batch, 1, keepdims=False)
    ids_col = active_blocks.reshape(owners, per_batch, SLOT_BLOCKS)
    counts_col = lax.dynamic_index_in_dim(block_counts, my_batch, 1, keepdims=False).reshape(
        owners, per_batch
    )
    lengths = passage_len.reshape(owners, per_batch)
    slot_ids, divisor, token_ok, col_ok = slot_info(
        onehot, ids_col, counts_col, lengths, plen_size, BLOCK
    )
    cot_col = rep_cot.reshape(owners, per_batch, col_width).astype(jnp.float32)
    slot_cot = jnp.einsum("jsp,jpc->jsc", onehot.astype(jnp.float32), cot_col)
    w_blocks = weights.reshape(OWN_BLOCKS, BLOCK, dslice)
    bias_blocks = bias.reshape(OWN_BLOCKS, BLOCK)
    bias_cols = bias_blocks[slot_ids].reshape(owners, OWN_SLOTS, col_width)

    def partial_for(inputs_here):
        slot_rows, block_ids = inputs_here
        w_sel = w_blocks[block_ids].reshape(OWN_SLOTS, col_width, dslice)
        return jnp.einsum(
            "std,scd->stc", slot_rows, w_sel, preferred_element_type=jnp.float32
        ).astype(jnp.bfloat16)

    partial_value = lax.map(partial_for, (arrived, slot_ids))
    my_share = owners // feature_parts
    my_start = lax.axis_index("dp") * my_share
    logits_mine = lax.psum_scatter(partial_value, "dp", scatter_dimension=0, tiled=True).astype(
        jnp.float32
    )
    pooled_mine, slope_mine = activate(
        logits_mine,
        lax.dynamic_slice_in_dim(bias_cols, my_start, my_share, 0),
        lax.dynamic_slice_in_dim(slot_cot, my_start, my_share, 0),
        lax.dynamic_slice_in_dim(token_ok, my_start, my_share, 0),
        lax.dynamic_slice_in_dim(col_ok, my_start, my_share, 0),
        lax.dynamic_slice_in_dim(divisor, my_start, my_share, 0),
    )
    slope_all = lax.all_gather(slope_mine, "dp", axis=0, tiled=True)

    def backward_step(grad_sum, inputs_here):
        slot_rows, block_ids, slope = inputs_here
        w_sel = w_blocks[block_ids].reshape(OWN_SLOTS, col_width, dslice)
        back_part = jnp.einsum(
            "stc,scd->std", slope, w_sel, preferred_element_type=jnp.float32
        ).astype(jnp.bfloat16)
        outer_sum = jnp.einsum("std,stc->scd", slot_rows, slope, preferred_element_type=jnp.float32)
        grad_sum = grad_sum.at[block_ids.reshape(-1)].add(
            outer_sum.reshape(OWN_SLOTS * SLOT_BLOCKS, BLOCK, dslice)
        )
        return (grad_sum, back_part)

    start_grad = jnp.zeros((OWN_BLOCKS, BLOCK, dslice), jnp.float32)
    grad_blocks, returned = lax.scan(backward_step, start_grad, (arrived, slot_ids, slope_all))
    back_home = lax.all_to_all(returned, "vocab", split_axis=0, concat_axis=0, tiled=True)
    gathered = jnp.dot(
        pick_rows.T,
        back_home.reshape(owners * OWN_SLOTS, plen_size * dslice),
        preferred_element_type=jnp.float32,
    )
    grad_hidden = gathered.reshape(per_batch, plen_size, dslice).astype(jnp.bfloat16)
    grad_w = grad_blocks.reshape(OWN_BLOCKS * BLOCK, dslice)
    new_first = (beta_one * first_moment.astype(jnp.float32) + (1.0 - beta_one) * grad_w).astype(
        jnp.bfloat16
    )
    new_second = (
        beta_two * second_moment.astype(jnp.float32) + (1.0 - beta_two) * grad_w * grad_w
    ).astype(jnp.bfloat16)
    reps = pooled_mine[:, None, :, :]
    return (reps, grad_hidden, new_first, new_second)


def solution(mesh):
    return jax.shard_map(
        shards,
        mesh=mesh,
        in_specs=(
            P("vocab", None, "dp"),
            P("vocab", "dp"),
            P("vocab"),
            P("vocab", "dp"),
            P("vocab", "dp"),
            P(None, "vocab", None),
            P(None, "vocab", None),
            P(),
            P(),
        ),
        out_specs=(
            P("dp", "vocab", None, None),
            P("vocab", None, "dp"),
            P("vocab", "dp"),
            P("vocab", "dp"),
        ),
        check_vma=False,
    )
```

profile of v0, /device:TPU:1, one launch (start us, length us, event | category | flops | bytes accessed | tf_op | source)
XLA Modules:
  0.0 653.2 jit_solution(12631458405986258486)
XLA Ops:
  15.3 10.1 %all-to-all-start = ((bf16[16,4,128,256]{3,2,1,0:T(8,128)(2,1)}), bf16[16,4,128,256]{3,2,1,0:T(8,128)(2,1)}, u32[]{:S(2)}, u32[]{:S(2)}) async-start(bf16[16,4,128,256]{3,2,1,0:T(8,128)(2,1)} %bitcast.132), calls=%async_computation | async-start | bytes 8388608 | tf_op jit(solution)/shard_map/all_to_all | solution.py:73
  27.6 91.4 %all-to-all-done = bf16[16,4,128,256]{3,2,1,0:T(8,128)(2,1)} async-done(((bf16[16,4,128,256]{3,2,1,0:T(8,128)(2,1)}), bf16[16,4,128,256]{3,2,1,0:T(8,128)(2,1)}, u32[]{:S(2)}, u32[]{:S(2)}) %all-to-all-start) | async-done | bytes 4194336 | tf_op jit(solution)/shard_map/all_to_all | solution.py:73
  119.0 78.0 %while.22 = (s32[]{:T(128)}, bf16[16,4,128,512]{2,3,1,0:T(8,128)(2,1)}, bf16[16,4,128,256]{3,2,1,0:T(8,128)(2,1)}, s32[16,4,4]{2,1,0:T(4,128)S(1)}, bf16[32,128,256]{2,1,0:T(8,128)(2,1)}, /*index=5*/s32[]{:T(128)}) while((s32[]{:T(128)}, bf16[16,4,128,512]{2,3,1,0:T(8,128)(2,1)}, bf16[16,4,128,256]{3,2,1,0:T(8,128)(2,1)}, ...), condition=%wide.region_3.4_spmd, body=%wide.region_2.3_spmd.sunk | while | flops 134480944 | bytes 6033881 | solution.py:96
  199.2 86.8 %reduce-scatter.4.cloned.1.call-done = bf16[1,4,128,512]{2,3,1,0:T(8,128)(2,1)} async-done(((bf16[16,4,128,512]{2,3,1,0:T(8,128)(2,1)}), bf16[1,4,128,512]{2,3,1,0:T(8,128)(2,1)}) %reduce-scatter.4.cloned.1.call-update) | async-done | bytes 524304
  291.0 76.7 %all-gather.2.cloned.1.call-done = bf16[16,4,128,512]{3,2,1,0:T(8,128)(2,1)} async-done(((bf16[1,4,128,512]{3,2,1,0:T(8,128)(2,1)}), bf16[16,4,128,512]{3,2,1,0:T(8,128)(2,1)}) %all-gather.2.cloned.1.call-update) | async-done | bytes 8388624 | tf_op jit(solution)/shard_map/all_gather | solution.py:110
  370.1 168.7 %while.23 = (s32[]{:T(128)}, f32[32,128,256]{2,1,0:T(8,128)}, bf16[16,4,128,256]{3,2,1,0:T(8,128)(2,1)}, s32[16,4,4]{2,1,0:T(4,128)S(1)}, bf16[16,4,128,512]{3,2...) while((s32[]{:T(128)}, f32[32,128,256]{2,1,0:T(8,128)}, ...), condition=%wide.region_11.12_spmd, body=%wide.region_9.11_spmd.sunk | while | flops 269091936 | bytes 13114209 | solution.py:125
  371.8 4.5 scatter_fusion
  382.4 4.4 scatter_fusion
  392.9 4.5 scatter_fusion
  403.4 4.5 scatter_fusion
  414.0 4.7 scatter_fusion
  424.8 4.5 scatter_fusion
  435.3 4.5 scatter_fusion
  445.9 4.4 scatter_fusion
  456.4 4.5 scatter_fusion
  477.4 4.5 scatter_fusion
  487.9 4.4 scatter_fusion
  498.4 4.5 scatter_fusion
  509.0 4.5 scatter_fusion
  519.5 4.5 scatter_fusion
  538.8 8.2 %all-to-all-start.1 = ((bf16[16,4,128,256]{3,2,1,0:T(8,128)(2,1)}), bf16[16,4,128,256]{3,2,1,0:T(8,128)(2,1)}, u32[]{:S(2)}, u32[]{:S(2)}) async-start(bf16[16,4,128,256]{3,2,1,0:T(8,128)(2,1)} %get-tuple-element.70), calls=%async_computation.1 | async-start | bytes 8388608 | tf_op jit(solution)/shard_map/all_to_all | solution.py:126
  547.0 6.3 fusion.17
  553.3 87.2 %all-to-all-done.1 = bf16[16,4,128,256]{3,2,1,0:T(8,128)(2,1)} async-done(((bf16[16,4,128,256]{3,2,1,0:T(8,128)(2,1)}), bf16[16,4,128,256]{3,2,1,0:T(8,128)(2,1)}, u32[]{:S(2)}, u32[]{:S(2)}) %all-to-all-start.1) | async-done | bytes 4194336 | tf_op jit(solution)/shard_map/all_to_all | solution.py:126
  640.5 4.5 fusion.23
  (295 shorter events, 204.2 us)
Async XLA Ops:
  7.2 191.7 %copy-start = (bf16[256,1,512]{2,0,1:T(8,128)(2,1)S(1)}, bf16[256,1,512]{2,0,1:T(8,128)(2,1)}, u32[]{:S(2)}) copy-start(bf16[256,1,512]{2,0,1:T(8,128)(2,1)} %param.18) | copy-start | bytes 786436
  15.3 10.2 %copy-start.3 = (s32[256,1,4]{0,2,1:T(4,128)S(1)}, s32[256,1,4]{0,2,1:T(4,128)}, u32[]{:S(2)}) copy-start(s32[256,1,4]{0,2,1:T(4,128)} %param.19) | copy-start | bytes 12292
  15.3 11.0 %copy-start.4 = (s32[256]{0:T(256)S(1)}, s32[256]{0:T(256)}, u32[]{:S(2)}) copy-start(s32[256]{0:T(256)} %param.21) | copy-start | bytes 3076
  15.3 103.6 %all-to-all-start = ((bf16[16,4,128,256]{3,2,1,0:T(8,128)(2,1)}), bf16[16,4,128,256]{3,2,1,0:T(8,128)(2,1)}, u32[]{:S(2)}, u32[]{:S(2)}) async-start(bf16[16,4,128,256]{3,2,1,0:T(8,128)(2,1)} %bitcast.132), calls=%async_computation | async-start | bytes 8388608 | tf_op jit(solution)/shard_map/all_to_all | solution.py:73
  25.4 260.5 %reduce-scatter.4.cloned.1.call-start = ((), (), s32[]{:S(2)}) async-start(), calls=%async_computation.4 | async-start | bytes 8912896
  196.9 0.7 copy-start.1
  197.0 170.7 %all-gather.2.cloned.1.call-start = ((), (), s32[]{:S(2)}) async-start(), calls=%async_computation.3 | async-start | bytes 8912896 | tf_op jit(solution)/shard_map/all_gather | solution.py:110
  538.8 8.3 %copy-start.2 = (bf16[4096,256]{1,0:T(8,128)(2,1)S(1)}, bf16[4096,256]{1,0:T(8,128)(2,1)}, u32[]{:S(2)}) copy-start(bf16[4096,256]{1,0:T(8,128)(2,1)} %param.17) | copy-start | bytes 6291460
  538.8 101.8 %all-to-all-start.1 = ((bf16[16,4,128,256]{3,2,1,0:T(8,128)(2,1)}), bf16[16,4,128,256]{3,2,1,0:T(8,128)(2,1)}, u32[]{:S(2)}, u32[]{:S(2)}) async-start(bf16[16,4,128,256]{3,2,1,0:T(8,128)(2,1)} %get-tuple-element.70), calls=%async_computation.1 | async-start | bytes 8388608 | tf_op jit(solution)/shard_map/all_to_all | solution.py:126
Sparse Core Ops, SparseCore 0:
  197.1 88.7 reduce-scatter.3
  291.1 76.5 all-gather.1
where the time goes:
time: 657 us; the launch traced here: 653 us
  waiting for transfers between devices  342 us (52%)
  local copies, waits for them, and re-layouts  105 us (16%)
  matrix products  87.3 us (13%)
  other arithmetic  85.5 us (13%)
  starting transfers between devices  18.4 us (3%)
  between operations  14.2 us (2%)
    all_to_all x1, waiting for transfers between devices, shards(): lax.all_to_all(outgoing, 'vocab', split_axis=0, concat_axis=0, tiled=True)  91.4 us
    all_to_all x1, waiting for transfers between devices, shards(): lax.all_to_all(returned, 'vocab', split_axis=0, concat_axis=0, tiled=True)  87.2 us
    unnamed x3, waiting for transfers between devices  86.8 us
    all_gather x1, waiting for transfers between devices, shards(): slope_all = lax.all_gather(slope_mine, 'dp', axis=0, tiled=True)  76.7 us
    scatter-add x16, other arithmetic, backward_step(): grad_sum.at[block_ids.reshape(-1)]  71.6 us
    gather x16, local copies, waits for them, and re-layouts, partial_for(): w_sel = w_blocks[block_ids].reshape(OWN_SLOTS, col_width, dslice)  35.3 us
    gather x16, local copies, waits for them, and re-layouts, backward_step(): w_sel = w_blocks[block_ids].reshape(OWN_SLOTS, col_width, dslice)  35.3 us
    dot_general x16, matrix products, backward_step(): jnp.einsum('stc,scd->std', slope, w_sel, preferred_element_type=jnp.float32)  33.1 us
  transfers between devices with their start and end apart: 4, of which 4 were waited for; matrix products, arithmetic and copies ran while one was open for 2% of the time, Pallas kernels for 0%

commit v1 on v0

v1 whole, which is shorter than its diff:
```python
import functools

import jax
import jax.numpy as jnp
from jax import lax
from jax.experimental import pallas as pl
from jax.experimental.pallas import tpu as pltpu
from jax.sharding import PartitionSpec as P

BLOCK = 128
OWN_BLOCKS = 32
SLOT_BLOCKS = 4
OWN_SLOTS = 4
TILE = 16
CAP_SHARE = 15
CAP_PARTS = 32

beta_one = 0.9
beta_two = 0.999

PASS, COUNT, ROWS, OFF, LEN, IDS = 0, 1, 2, 3, 4, 5
WIDTH = 16
UNIT, START, TLEN, BIAS_ROW, COT_ROW = 0, 1, 2, 3, 4
TWIDTH = 8

CONTRACT_LAST = (((1,), (1,)), ((), ()))
CONTRACT_FIRST = (((0,), (0,)), ((), ()))


def slot_table(counts_all, ids, lengths, me):
    batches, per_batch, owners = counts_all.shape
    live = (counts_all > 0).astype(jnp.int32)
    place = jnp.arange(per_batch, dtype=jnp.int32)
    earlier = (place[None, :] < place[:, None]).astype(jnp.int32)
    rank = jnp.sum(live[:, None, :, :] * earlier[None, :, :, None], axis=2)
    slot_place = jnp.arange(OWN_SLOTS, dtype=jnp.int32)
    padded = (lengths + TILE - 1) // TILE * TILE
    kept = live * (rank < OWN_SLOTS)
    totals = jnp.sum(kept * counts_all * padded[:, :, None], axis=(0, 1))
    counts = lax.dynamic_index_in_dim(counts_all, me, 2, keepdims=False)
    live_me = lax.dynamic_index_in_dim(live, me, 2, keepdims=False)
    rank_me = lax.dynamic_index_in_dim(rank, me, 2, keepdims=False)
    chosen = (
        (live_me[:, None, :] == 1) & (rank_me[:, None, :] == slot_place[None, :, None])
    ).astype(jnp.int32)
    first = jnp.arange(batches, dtype=jnp.int32)[:, None] * per_batch
    passage = jnp.sum(chosen * place[None, None, :], axis=2) + first
    count = jnp.sum(chosen * counts[:, None, :], axis=2)
    length = jnp.sum(chosen * lengths[:, None, :], axis=2)
    rows = jnp.sum(chosen * padded[:, None, :], axis=2)
    slot_ids = jnp.sum(chosen[:, :, :, None] * ids[:, None, :, :], axis=2)
    slots = batches * OWN_SLOTS
    need = (count * rows).reshape(slots)
    order = jnp.arange(slots, dtype=jnp.int32)
    off = jnp.sum(jnp.where(order[None, :] < order[:, None], need[None, :], 0), axis=1)
    columns = [
        passage.reshape(slots, 1),
        count.reshape(slots, 1),
        rows.reshape(slots, 1),
        off.reshape(slots, 1),
        length.reshape(slots, 1),
        slot_ids.reshape(slots, SLOT_BLOCKS),
        jnp.zeros((slots, WIDTH - IDS - SLOT_BLOCKS), jnp.int32),
    ]
    return jnp.concatenate(columns, axis=1), jnp.max(totals)


def tile_table(slots, first_tile, tiles):
    at = first_tile + jnp.arange(tiles, dtype=jnp.int32)
    starts = slots[:, OFF] // TILE
    holder = jnp.sum((starts[None, :] <= at[:, None]).astype(jnp.int32), axis=1) - 1
    order = jnp.arange(slots.shape[0], dtype=jnp.int32)
    pick = (holder[:, None] == order[None, :]).astype(jnp.int32)
    mine = jnp.sum(pick[:, :, None] * slots[None, :, :], axis=1)
    height = mine[:, ROWS] // TILE
    rel = at - mine[:, OFF] // TILE
    q = sum((rel >= height * n).astype(jnp.int32) for n in range(1, SLOT_BLOCKS))
    start = (rel - q * height) * TILE
    length = jnp.where(rel < height * mine[:, COUNT], mine[:, LEN], 0)
    which = jnp.arange(SLOT_BLOCKS, dtype=jnp.int32)
    block = jnp.sum(
        jnp.where(which[None, :] == q[:, None], mine[:, IDS : IDS + SLOT_BLOCKS], 0), axis=1
    )
    columns = [
        holder * SLOT_BLOCKS + q,
        start,
        length,
        block,
        mine[:, PASS] * SLOT_BLOCKS + q,
    ]
    filler = jnp.zeros((tiles,), jnp.int32)
    return jnp.stack(columns + [filler] * (TWIDTH - len(columns)), axis=1).reshape(-1)


def pair_weights(w_ref, tab_ref, base, pair):
    one = tab_ref[base + IDS + 2 * pair]
    two = tab_ref[base + IDS + 2 * pair + 1]
    return jnp.concatenate([w_ref[one], w_ref[two]], axis=0)


def pair_slopes(buf, tab_ref, base, pair):
    plen = BLOCK
    count, rows = tab_ref[base + COUNT], tab_ref[base + ROWS]
    off, length = tab_ref[base + OFF], tab_ref[base + LEN]
    token = lax.broadcasted_iota(jnp.int32, (plen, BLOCK), 0)
    halves = []
    for q in (2 * pair, 2 * pair + 1):
        at = pl.multiple_of(off + q * rows, TILE)
        value = buf[pl.ds(at, plen), :]
        bound = jnp.where(q < count, length, 0)
        halves.append(jnp.where(token < bound, value.astype(jnp.float32), 0.0).astype(jnp.bfloat16))
    return jnp.concatenate(halves, axis=1)


def forward_kernel(cap, tab_ref, *refs):
    hidden_refs, w_ref = refs[:OWN_SLOTS], refs[OWN_SLOTS]
    main_ref, rest_ref, buf, sems = refs[OWN_SLOTS + 1 :]
    j = pl.program_id(0)
    for s in range(OWN_SLOTS):
        base = (j * OWN_SLOTS + s) * WIDTH
        count, rows, off = tab_ref[base + COUNT], tab_ref[base + ROWS], tab_ref[base + OFF]
        for pair in range(SLOT_BLOCKS // 2):

            @pl.when(count > 2 * pair)
            def _():
                w2 = pair_weights(w_ref, tab_ref, base, pair)
                value = lax.dot_general(
                    hidden_refs[s][0], w2, CONTRACT_LAST, preferred_element_type=jnp.float32
                ).astype(jnp.bfloat16)
                at = pl.multiple_of(off + 2 * pair * rows, TILE)
                buf[pl.ds(at, BLOCK), :] = value[:, :BLOCK]
                at = pl.multiple_of(off + (2 * pair + 1) * rows, TILE)
                buf[pl.ds(at, BLOCK), :] = value[:, BLOCK:]

    last = pl.num_programs(0) - 1

    @pl.when(j == last)
    def _():
        copy = pltpu.make_async_copy(buf.at[pl.ds(0, cap)], main_ref, sems.at[0])
        copy.start()
        copy.wait()
        base = (last * OWN_SLOTS + OWN_SLOTS - 1) * WIDTH
        total = tab_ref[base + OFF] + tab_ref[base + COUNT] * tab_ref[base + ROWS]

        @pl.when(total > cap)
        def _():
            more = pltpu.make_async_copy(
                buf.at[pl.ds(cap, rest_ref.shape[0])], rest_ref, sems.at[1]
            )
            more.start()
            more.wait()


def activate_kernel(tiles, tile_ref, lg_ref, bias_ref, cot_ref, slope_ref, pooled_ref):
    pooled_ref[...] = jnp.zeros_like(pooled_ref)

    def step(i, carry):
        base = i * TWIDTH
        unit, start = tile_ref[base + UNIT], tile_ref[base + START]
        length, bias_row = tile_ref[base + TLEN], tile_ref[base + BIAS_ROW]
        cot_row = tile_ref[base + COT_ROW]
        at = pl.multiple_of(i * TILE, TILE)
        x = lg_ref[pl.ds(at, TILE), :].astype(jnp.float32) + bias_ref[pl.ds(bias_row, 1), :]
        token = lax.broadcasted_iota(jnp.int32, x.shape, 0) + start
        keep = token < length
        divisor = jnp.full((1, BLOCK), jnp.maximum(length, 1), jnp.int32).astype(jnp.float32)
        weight = 1.0 / divisor
        small = jnp.exp(-jnp.abs(x))
        soft = jnp.maximum(x, 0.0) + jnp.log1p(small)
        sig = jnp.where(x >= 0, 1.0, small) / (1.0 + small)
        gain = jnp.where(keep, jnp.log1p(soft) * weight, 0.0)
        pooled_ref[pl.ds(unit, 1), :] += jnp.sum(gain, axis=0, keepdims=True)
        cot = cot_ref[pl.ds(cot_row, 1), :] * weight
        slope = jnp.where(keep, cot * sig / (1.0 + soft), 0.0)
        slope_ref[pl.ds(at, TILE), :] = slope.astype(jnp.bfloat16)
        return carry

    lax.fori_loop(0, tiles, step, 0, unroll=4)


def load_slopes(cap, tab_ref, main_ref, rest_ref, buf, sems, slots):
    copy = pltpu.make_async_copy(main_ref, buf.at[pl.ds(0, cap)], sems.at[0])
    copy.start()
    copy.wait()
    base = (slots - 1) * WIDTH
    total = tab_ref[base + OFF] + tab_ref[base + COUNT] * tab_ref[base + ROWS]

    @pl.when(total > cap)
    def _():
        more = pltpu.make_async_copy(rest_ref, buf.at[pl.ds(cap, rest_ref.shape[0])], sems.at[1])
        more.start()
        more.wait()


def hidden_grad_kernel(cap, tab_ref, main_ref, rest_ref, w_ref, out_ref, buf, sems):
    j = pl.program_id(0)

    @pl.when(j == 0)
    def _():
        load_slopes(cap, tab_ref, main_ref, rest_ref, buf, sems, pl.num_programs(0) * OWN_SLOTS)

    out_ref[...] = jnp.zeros_like(out_ref)
    per_batch = out_ref.shape[0]
    for s in range(OWN_SLOTS):
        base = (j * OWN_SLOTS + s) * WIDTH
        count = tab_ref[base + COUNT]
        local = tab_ref[base + PASS] - j * per_batch

        @pl.when((count > 0) & (count <= 2))
        def _():
            slopes = pair_slopes(buf, tab_ref, base, 0)
            w2 = pair_weights(w_ref, tab_ref, base, 0)
            value = jnp.dot(slopes, w2, preferred_element_type=jnp.float32)
            out_ref[local] = value.astype(jnp.bfloat16)

        @pl.when(count > 2)
        def _():
            slopes = jnp.concatenate(
                [pair_slopes(buf, tab_ref, base, 0), pair_slopes(buf, tab_ref, base, 1)], axis=1
            )
            w4 = jnp.concatenate(
                [pair_weights(w_ref, tab_ref, base, 0), pair_weights(w_ref, tab_ref, base, 1)],
                axis=0,
            )
            value = jnp.dot(slopes, w4, preferred_element_type=jnp.float32)
            out_ref[local] = value.astype(jnp.bfloat16)


def weight_grad_kernel(cap, batches, tab_ref, *refs):
    hidden_refs = refs[:OWN_SLOTS]
    main_ref, rest_ref, m_ref, v_ref, first_ref, second_ref, buf, acc, sems = refs[OWN_SLOTS:]
    i = pl.program_id(0)

    @pl.when(i == 0)
    def _():
        load_slopes(cap, tab_ref, main_ref, rest_ref, buf, sems, batches * OWN_SLOTS)
        acc[...] = jnp.zeros_like(acc)

    @pl.when(i < batches)
    def _():
        for s in range(OWN_SLOTS):
            base = (i * OWN_SLOTS + s) * WIDTH
            count = tab_ref[base + COUNT]
            for pair in range(SLOT_BLOCKS // 2):

                @pl.when(count > 2 * pair)
                def _():
                    slopes = pair_slopes(buf, tab_ref, base, pair)
                    value = lax.dot_general(
                        slopes,
                        hidden_refs[s][0],
                        CONTRACT_FIRST,
                        preferred_element_type=jnp.float32,
                    )
                    acc[tab_ref[base + IDS + 2 * pair]] += value[:BLOCK]
                    acc[tab_ref[base + IDS + 2 * pair + 1]] += value[BLOCK:]

    @pl.when(i >= batches)
    def _():
        group = m_ref.shape[0]
        at = (i - batches) * group
        grad = acc[pl.ds(at, group)]
        m = m_ref[...].astype(jnp.float32)
        v = v_ref[...].astype(jnp.float32)
        first_ref[...] = (beta_one * m + (1.0 - beta_one) * grad).astype(jnp.bfloat16)
        second_ref[...] = (beta_two * v + (1.0 - beta_two) * grad * grad).astype(jnp.bfloat16)


def shards(
    hidden,
    weights,
    bias,
    first_moment,
    second_moment,
    rep_cot,
    active_blocks,
    block_counts,
    passage_len,
):
    batches = lax.axis_size("vocab")
    parts = lax.axis_size("dp")
    per_batch, plen, dslice = hidden.shape
    col_width = SLOT_BLOCKS * BLOCK
    slots = batches * OWN_SLOTS
    full = slots * SLOT_BLOCKS * plen
    cap = full * CAP_SHARE // CAP_PARTS
    rest = full - cap
    slack = 2 * BLOCK
    me = lax.axis_index("vocab")
    rank = lax.axis_index("dp")

    rows_all = lax.all_gather(hidden, "vocab", axis=0, tiled=True)

    table, most = slot_table(
        block_counts.reshape(batches, per_batch, batches),
        active_blocks.reshape(batches, per_batch, SLOT_BLOCKS),
        passage_len.reshape(batches, per_batch),
        me,
    )
    tab = table.reshape(-1)
    cot_rows = rep_cot.astype(jnp.float32).reshape(-1, BLOCK)
    bias_rows = bias.reshape(OWN_BLOCKS, BLOCK)
    w_blocks = weights.reshape(OWN_BLOCKS, BLOCK, dslice)

    any_spec = pl.BlockSpec(memory_space=pl.ANY)
    vmem = pl.BlockSpec(memory_space=pltpu.VMEM)
    smem = pl.BlockSpec(memory_space=pltpu.SMEM)

    def passage_spec(s):
        def index(i, t):
            row = jnp.minimum(i, batches - 1) * OWN_SLOTS + s
            return (t[row * WIDTH + PASS], 0, 0)

        return pl.BlockSpec((1, plen, dslice), index)

    passage_specs = [passage_spec(s) for s in range(OWN_SLOTS)]
    w_spec = pl.BlockSpec(
        w_blocks.shape, lambda i, t: (0, 0, 0), pipeline_mode=pl.Buffered(buffer_count=1)
    )
    buf_shape = pltpu.VMEM((full + slack, BLOCK), jnp.bfloat16)
    sems = pltpu.SemaphoreType.DMA((2,))
    limit = 60 * 1024 * 1024
    flops = 2 * slots * plen * col_width * dslice

    main, over = pl.pallas_call(
        functools.partial(forward_kernel, cap),
        out_shape=(
            jax.ShapeDtypeStruct((cap, BLOCK), jnp.bfloat16),
            jax.ShapeDtypeStruct((rest, BLOCK), jnp.bfloat16),
        ),
        grid_spec=pltpu.PrefetchScalarGridSpec(
            num_scalar_prefetch=1,
            grid=(batches,),
            in_specs=passage_specs + [w_spec],
            out_specs=(any_spec, any_spec),
            scratch_shapes=[buf_shape, sems],
        ),
        compiler_params=pltpu.CompilerParams(vmem_limit_bytes=limit),
        cost_estimate=pl.CostEstimate(
            flops=flops, bytes_accessed=16 * 1024 * 1024, transcendentals=0
        ),
        name="forward",
    )(tab, *([rows_all] * OWN_SLOTS), w_blocks)

    def exchange(packed, first_row):
        mine = lax.psum_scatter(packed, "dp", scatter_dimension=0, tiled=True)
        height = packed.shape[0] // parts
        tiles = height // TILE
        places = tile_table(table, (first_row + rank * height) // TILE, tiles)
        slope_mine, pooled = pl.pallas_call(
            functools.partial(activate_kernel, tiles),
            out_shape=(
                jax.ShapeDtypeStruct((height, BLOCK), jnp.bfloat16),
                jax.ShapeDtypeStruct((slots * SLOT_BLOCKS, BLOCK), jnp.float32),
            ),
            in_specs=[smem, vmem, vmem, vmem],
            out_specs=(vmem, vmem),
            name="activate",
        )(places, mine, bias_rows, cot_rows)
        return lax.all_gather(slope_mine, "dp", axis=0, tiled=True), pooled

    slopes, pooled = exchange(main, 0)
    slopes_over, pooled_over = lax.cond(
        most > cap,
        lambda packed: exchange(packed, cap),
        lambda packed: (jnp.zeros_like(packed), jnp.zeros_like(pooled)),
        over,
    )
    pooled = pooled + pooled_over

    grads_all = pl.pallas_call(
        functools.partial(hidden_grad_kernel, cap),
        out_shape=jax.ShapeDtypeStruct((batches * per_batch, plen, dslice), jnp.bfloat16),
        grid_spec=pltpu.PrefetchScalarGridSpec(
            num_scalar_prefetch=1,
            grid=(batches,),
            in_specs=[any_spec, any_spec, w_spec],
            out_specs=pl.BlockSpec((per_batch, plen, dslice), lambda i, t: (i, 0, 0)),
            scratch_shapes=[buf_shape, sems],
        ),
        compiler_params=pltpu.CompilerParams(vmem_limit_bytes=limit),
        cost_estimate=pl.CostEstimate(
            flops=flops, bytes_accessed=24 * 1024 * 1024, transcendentals=0
        ),
        name="hidden_grad",
    )(tab, slopes, slopes_over, w_blocks)
    grad_hidden = lax.psum_scatter(grads_all, "vocab", scatter_dimension=0, tiled=True)

    pooled_parts = lax.all_to_all(
        pooled.reshape(parts, -1, BLOCK), "dp", split_axis=0, concat_axis=0, tiled=True
    )
    reps = jnp.sum(pooled_parts, axis=0).reshape(1, 1, OWN_SLOTS, col_width)

    group = 4
    moment_spec = pl.BlockSpec(
        (group, BLOCK, dslice), lambda i, t: (jnp.maximum(i - batches, 0), 0, 0)
    )
    moment_shape = jax.ShapeDtypeStruct((OWN_BLOCKS, BLOCK, dslice), jnp.bfloat16)
    new_first, new_second = pl.pallas_call(
        functools.partial(weight_grad_kernel, cap, batches),
        out_shape=(moment_shape, moment_shape),
        grid_spec=pltpu.PrefetchScalarGridSpec(
            num_scalar_prefetch=1,
            grid=(batches + OWN_BLOCKS // group,),
            in_specs=passage_specs + [any_spec, any_spec, moment_spec, moment_spec],
            out_specs=(moment_spec, moment_spec),
            scratch_shapes=[buf_shape, pltpu.VMEM((OWN_BLOCKS, BLOCK, dslice), jnp.float32), sems],
        ),
        compiler_params=pltpu.CompilerParams(vmem_limit_bytes=limit),
        cost_estimate=pl.CostEstimate(
            flops=flops, bytes_accessed=24 * 1024 * 1024, transcendentals=0
        ),
        name="weight_grad",
    )(
        tab,
        *([rows_all] * OWN_SLOTS),
        slopes,
        slopes_over,
        first_moment.reshape(moment_shape.shape),
        second_moment.reshape(moment_shape.shape),
    )
    return (
        reps,
        grad_hidden,
        new_first.reshape(first_moment.shape),
        new_second.reshape(second_moment.shape),
    )


def solution(mesh):
    return jax.shard_map(
        shards,
        mesh=mesh,
        in_specs=(
            P("vocab", None, "dp"),
            P("vocab", "dp"),
            P("vocab"),
            P("vocab", "dp"),
            P("vocab", "dp"),
            P(None, "vocab", None),
            P(None, "vocab", None),
            P(),
            P(),
        ),
        out_specs=(
            P("dp", "vocab", None, None),
            P("vocab", None, "dp"),
            P("vocab", "dp"),
            P("vocab", "dp"),
        ),
        check_vma=False,
    )
```

time: 657 us -> 405 us (0.62)
  local copies, waits for them, and re-layouts: 105 us -> 12 us
  matrix products: 87.3 us -> 0 us
  other arithmetic: 85.5 us -> 5.33 us
  Pallas kernels: 0 us -> 75.7 us
  waiting for transfers between devices: 342 us -> 283 us
  starting transfers between devices: 18.4 us -> 0.12 us
  blocking collectives: 0 us -> 11.6 us
    all_to_all x2 -> x0, waiting for transfers between devices: 179 us -> none  [the longest x1 91.4 us: shards(): lax.all_to_all(outgoing, 'vocab', split_axis=0, concat_axis=0, tiled=True)]
    reduce_scatter x0 -> x2, waiting for transfers between devices: none -> 134 us  [the longest x1 80.2 us: exchange(): mine = lax.psum_scatter(packed, 'dp', scatter_dimension=0, tiled=True)]
    dot_general x51 -> x0, matrix products: 87.3 us -> none  [the longest x16 33.1 us: backward_step(): jnp.einsum('stc,scd->std', slope, w_sel, preferred_element_type=jnp.float32)]
    unnamed x3 -> x4, waiting for transfers between devices: 86.8 us -> 1.44 us
    pallas_call x0 -> x4, Pallas kernels: none -> 75.7 us  [the longest x1 31.5 us: shards(): pl.pallas_call(functools.partial(weight_grad_kernel, cap, batches), out_s...]
    scatter-add x16 -> x0, other arithmetic: 71.6 us -> none  [backward_step(): grad_sum.at[block_ids.reshape(-1)]]
    gather x33 -> x0, local copies, waits for them, and re-layouts: 71.3 us -> none  [the longest x16 35.3 us: partial_for(): w_sel = w_blocks[block_ids].reshape(OWN_SLOTS, col_width, dslice)]
    all_gather x1 -> x2, waiting for transfers between devices: 76.7 us -> 147 us  [the longest x1 91 us: shards(): rows_all = lax.all_gather(hidden, 'vocab', axis=0, tiled=True)]
  transfers between devices with their start and end apart: 4 -> 4, of which waited for: 4 -> 4; matrix products, arithmetic and copies ran while one was open for 2% -> 3% of each run, Pallas kernels for 0% -> 8%
where the time goes in v1:
time: 405 us; the launch traced here: 402 us
  waiting for transfers between devices  283 us (70%)
  Pallas kernels  75.7 us (19%)
  between operations  14.7 us (4%)
  local copies, waits for them, and re-layouts  12 us (3%)
  blocking collectives  11.6 us (3%)
  other arithmetic  5.33 us (1%)
    all_gather x1, waiting for transfers between devices, shards(): rows_all = lax.all_gather(hidden, 'vocab', axis=0, tiled=True)  91 us
    reduce_scatter x1, waiting for transfers between devices, exchange(): mine = lax.psum_scatter(packed, 'dp', scatter_dimension=0, tiled=True)  80.2 us
    all_gather x1, waiting for transfers between devices, exchange(): return (lax.all_gather(slope_mine, 'dp', axis=0, tiled=True), pooled)  56.1 us
    reduce_scatter x1, waiting for transfers between devices, shards(): lax.psum_scatter(grads_all, 'vocab', scatter_dimension=0, tiled=True)  54.2 us
    pallas_call x1, Pallas kernels, shards(): pl.pallas_call(functools.partial(weight_grad_kernel, cap, batches), out_s...  31.5 us
    pallas_call x1, Pallas kernels, shards(): pl.pallas_call(functools.partial(forward_kernel, cap), out_shape=(jax.Sha...  22.6 us
    pallas_call x1, Pallas kernels, shards(): pl.pallas_call(functools.partial(hidden_grad_kernel, cap), out_shape=jax....  18.7 us
    all_to_all x1, blocking collectives, shards(): lax.all_to_all(pooled.reshape(parts, -1, BLOCK), 'dp', split_axis=0, conc...  11.6 us
  transfers between devices with their start and end apart: 4, of which 4 were waited for; matrix products, arithmetic and copies ran while one was open for 3% of the time, Pallas kernels for 8%

profile of v1, /device:TPU:1, one launch (start us, length us, event | category | flops | bytes accessed | tf_op | source)
XLA Modules:
  0.0 402.5 jit_solution(2156592000483785015)
XLA Ops:
  7.2 0.7 all-gather.6.cloned.1.call-update
  7.9 0.8 reshape.311
  8.7 0.8 reshape.310
  9.6 0.6 multiply_reduce_fusion.1
  11.3 0.8 mul.255
  12.2 0.7 fusion.15
  12.9 0.8 multiply_reduce_fusion.4
  16.6 0.7 reshape.318.tab_ref
  17.3 1.1 reshape.330.cot_ref
  18.4 91.0 %all-gather.6.cloned.1.call-done.refs_0_.refs_1_.refs_2_.refs_3_ = bf16[256,128,256]{2,1,0:T(8,128)(2,1)} async-done(((bf16[16,128,256]{2,1,0:T(8,128)(2,1)}), bf16[256,128,256]{2,1,0:T(8,128)(2,1)}) %all-gather.6.cloned.1.call-update) | async-done | bytes 16777232 | tf_op jit(solution)/shard_map/all_gather | solution.py:292
  109.4 22.6 %forward.1 = (bf16[15360,128]{1,0:T(8,128)(2,1)}, bf16[17408,128]{1,0:T(8,128)(2,1)}) custom-call(s32[1024]{0:T(1024)} %reshape.318.tab_ref, bf16[256,128,256]{2,1,0:T(8,128)(2,1)} %all-gather.6.cloned.1.call-done.refs_0_.refs_1_.refs_2_.refs_3_, bf16[256,128,256]{2,1,0:T(8,128)(2,1)} %all-gather.6.cloned.1.call-done.refs_0_.refs_1_.refs_2_.refs_3_, ...), custom_call_target="tpu_custom_call" | custom-call | flops 2147483648 | bytes 16777216 | tf_op jit(solution)/shard_map/forward/pallas_call | solution.py:325
  132.0 2.7 conditional.1
  132.0 2.7 broadcast.477
  134.7 0.7 reduce-scatter.6.cloned.1.call-update
  135.8 1.1 multiply_reduce_fusion.2
  138.3 0.7 reshape.317.tile_ref
  139.0 80.2 %reduce-scatter.6.cloned.1.call-done.lg_ref = bf16[960,128]{1,0:T(8,128)(2,1)} async-done(((bf16[15360,128]{1,0:T(8,128)(2,1)}), bf16[960,128]{1,0:T(8,128)(2,1)}) %reduce-scatter.6.cloned.1.call-update) | async-done | bytes 245776 | tf_op jit(solution)/shard_map/reduce_scatter | solution.py:346
  219.2 2.9 activate.3
  222.1 56.1 %all-gather.8.cloned.1.call-done.main_ref.refs_4_ = bf16[15360,128]{1,0:T(8,128)(2,1)} async-done(((bf16[960,128]{1,0:T(8,128)(2,1)}), bf16[15360,128]{1,0:T(8,128)(2,1)}) %all-gather.8.cloned.1.call-update) | async-done | bytes 3932176 | tf_op jit(solution)/shard_map/all_gather | solution.py:360
  278.3 18.7 %hidden_grad.1 = bf16[256,128,256]{2,1,0:T(8,128)(2,1)} custom-call(s32[1024]{0:T(1024)} %reshape.318.tab_ref, bf16[15360,128]{1,0:T(8,128)(2,1)} %all-gather.8.cloned.1.call-done.main_ref.refs_4_, bf16[17408,128]{1,0:T(8,128)(2,1)} %get-tuple-element.37.rest_ref.refs_5_, bf16[32,128,256]{2,1,0:T(8,128)(2,1)} %bitcast.30), custom_call_target="tpu_custom_call" | custom-call | flops 2147483648 | bytes 25165824 | tf_op jit(solution)/shard_map/hidden_grad/pallas_call | solution.py:371
  297.1 0.9 copy-done
  297.9 11.6 %all_to_all.5 = f32[16,16,128]{2,1,0:T(8,128)S(1)} all-to-all(f32[16,16,128]{2,1,0:T(8,128)S(1)} %bitcast.33), channel_id=1, replica_groups=mesh['dp'=16,'vocab'=16] {'dp'}, dimensions={0} | all-to-all | bytes 262144 | tf_op jit(solution)/shard_map/all_to_all | solution.py:389
  310.2 31.5 %weight_grad.1 = (bf16[32,128,256]{2,1,0:T(8,128)(2,1)}, bf16[32,128,256]{2,1,0:T(8,128)(2,1)}) custom-call(s32[1024]{0:T(1024)} %reshape.318.tab_ref, bf16[256,128,256]{2,1,0:T(8,128)(2,1)} %all-gather.6.cloned.1.call-done.refs_0_.refs_1_.refs_2_.refs_3_, bf16[256,128,256]{2,1,0:T(8,128)(2,1)} %all-gather.6.cloned.1.call-done.refs_0_.refs_1_.refs_2_.refs_3_, ...), custom_call_target="tpu_custom_call" | custom-call | flops 2147483648 | bytes 25165824 | tf_op jit(solution)/shard_map/weight_grad/pallas_call | solution.py:399
  341.7 54.2 %reduce-scatter.8.cloned.1.call-done = bf16[16,128,256]{2,1,0:T(8,128)(2,1)} async-done(((bf16[256,128,256]{2,1,0:T(8,128)(2,1)}), bf16[16,128,256]{2,1,0:T(8,128)(2,1)}) %reduce-scatter.8.cloned.1.call-update) | async-done | bytes 1048592 | tf_op jit(solution)/shard_map/reduce_scatter | solution.py:387
  (67 shorter events, 5.9 us)
Async XLA Ops:
  7.2 102.2 %all-gather.6.cloned.1.call-start = ((), (), s32[]{:S(2)}) async-start(), calls=%async_computation.6 | async-start | bytes 17825792 | tf_op jit(solution)/shard_map/all_gather | solution.py:292
  109.4 22.6 %copy-start.1 = (f32[4096]{0:T(1024)S(1)}, f32[4096]{0:T(1024)}, u32[]{:S(2)}) copy-start(f32[4096]{0:T(1024)} %param.13) | copy-start | bytes 49156
  134.7 84.5 %reduce-scatter.6.cloned.1.call-start = ((), (), s32[]{:S(2)}) async-start(), calls=%async_computation.7 | async-start | bytes 4177920 | tf_op jit(solution)/shard_map/reduce_scatter | solution.py:346
  135.4 142.9 %all-gather.8.cloned.1.call-start = ((), (), s32[]{:S(2)}) async-start(), calls=%async_computation.8 | async-start | bytes 4177920 | tf_op jit(solution)/shard_map/all_gather | solution.py:360
  222.1 173.8 %reduce-scatter.8.cloned.1.call-start = ((), (), s32[]{:S(2)}) async-start(), calls=%async_computation.9 | async-start | bytes 17825792 | tf_op jit(solution)/shard_map/reduce_scatter | solution.py:387
  297.0 0.9 copy-start
Sparse Core Ops, SparseCore 0:
  9.8 99.5 all-gather.5
  139.2 79.9 reduce-scatter.5
  222.2 56.0 all-gather.7
  297.2 98.6 reduce-scatter.7
